TPU v7x, 512 devices: a whole 4x8x8 slice. The times are simulated.
512 devices in a mesh: seq: 32 (over y, z_lo, core), row: 4 (over x), col: 4 (over z_hi).
Axes of the slice: x: 4, y: 8, z: 8 (z_hi: 4, z_lo: 2; z = z_hi * 2 + z_lo), core: 2. Of those that a mesh axis runs over, the one named last changes fastest.
Arguments:
- hidden_in: bfloat16 [4, 16384, 1024], P('row', 'seq')
- qkv_weight: bfloat16 [1024, 16, 192], P(None, 'col'), may hold values from -0.1875 to 0.1875
- qkv_global_weight: bfloat16 [1024, 16, 192], P('row', 'col'), may hold values from -0.1875 to 0.1875
- out_weight: bfloat16 [1024, 1024], P('col'), may hold values from -0.75 to 0.75
- ln_gain: float32 [1024], replicated, may hold values from 0.1 to 1.9
- ln_bias: float32 [1024], replicated, may hold values from -3 to 3
- ffn_in: bfloat16 [1024, 4096], P('row', 'col'), may hold values from -0.1875 to 0.1875
- ffn_out: bfloat16 [4096, 1024], P('col', 'row'), may hold values from -0.09375 to 0.09375
- ln2_gain: float32 [1024], replicated, may hold values from 0.1 to 1.9
- ln2_bias: float32 [1024], replicated, may hold values from -3 to 3
- segment_ids: int32 [4, 16384], P('row'), may hold values from 0 to 63, never falling along the last dimension, each value on 1 to 9216 neighbouring positions
- global_pos: int32 [4, 128], P('row'), may hold values from 0 to 16383, as said below
- page_owner: int32 [4, 1024, 1], P('row', 'seq'), may hold values from 0 to 31; in each aligned block of 32 rows (0 to 31, 32 to 63, ..., all dimensions but the last counted through in order) at most 2 rows name the same one
Outputs:
- hidden_out: bfloat16 [4, 16384, 1024], P('row', ('seq', 'col'))
- page_pool: bfloat16 [4, 32, 32, 2, 16, 16, 128], P('row', 'seq', None, None, None, 'col')
Inputs may be any that keep to these rules, and one draw needn't show every extreme that they name: `segment_ids`: in each stream, prompt numbers never fall along positions and every prompt has 1 to 9216 tokens, one exactly 9216. `global_pos`: in each stream, exactly 4 distinct global positions lie in each block of 512 consecutive tokens, listed in increasing order. `page_owner`: among the 32 pages of one shard of a stream, at most 2 have the same owner.
All inputs are finite; a program needn't handle non-finite values.
Results may differ from a plain program's by a relative error of at most 0.014.
The roundings to bfloat16 on the way count: a program that leaves them out, or rounds other values in their place, can miss the bound.
Values may be sent and summed in bfloat16 or wider, within the bound.
A program may use at most 64 MiB of HBM per device.

v0:
```python
import math
import jax
import jax.numpy as jnp
from jax import lax
from jax.sharding import PartitionSpec as P

HALF = 256


def padded(block, sides, width):
    for axis, dim in sides:
        count = lax.axis_size(axis)
        forward = [(i, i + 1) for i in range(count - 1)]
        backward = [(target, source) for source, target in forward]
        low = lax.ppermute(
            lax.slice_in_dim(block, block.shape[dim] - width, None, axis=dim), axis, forward
        )
        high = lax.ppermute(lax.slice_in_dim(block, 0, width, axis=dim), axis, backward)
        block = jnp.concatenate([low, block, high], axis=dim)
    return block


def layer_norm(values, gain, bias):
    center = values - jnp.mean(values, axis=1, keepdims=True)
    spread = jnp.mean(center * center, axis=1, keepdims=True)
    return center * lax.rsqrt(spread + 1e-05) * gain + bias


def per_device(
    hidden_in,
    qkv_weight,
    qkv_global_weight,
    out_weight,
    ln_gain,
    ln_bias,
    ffn_in,
    ffn_out,
    ln2_gain,
    ln2_bias,
    segment_ids,
    global_pos,
    page_owner,
):
    neg = -1e30
    tokens = hidden_in[0]
    shard_len, width = tokens.shape
    heads_here = qkv_weight.shape[1]
    triple = qkv_weight.shape[2]
    head_dim = triple // 3
    n_seq = lax.axis_size("seq")
    n_row = lax.axis_size("row")
    n_col = lax.axis_size("col")
    seq_index = lax.axis_index("seq")
    col_index = lax.axis_index("col")
    base = seq_index * shard_len
    scale = 1.0 / math.sqrt(head_dim)
    all_pos = global_pos[0]
    n_glob = all_pos.shape[0]
    per_shard = n_glob // n_seq
    own_pos = lax.dynamic_slice_in_dim(all_pos, seq_index * per_shard, per_shard, 0)
    local_order = jnp.arange(shard_len, dtype=jnp.int32)
    own_match = (own_pos - base)[:, None] == local_order[None, :]
    picker = own_match.astype(jnp.bfloat16)
    own_rows = jnp.dot(picker, tokens, preferred_element_type=jnp.float32).astype(jnp.bfloat16)
    glob_rows = lax.all_gather(own_rows, "seq", axis=0, tiled=True)
    wg_rows = qkv_global_weight.shape[0]
    fi_rows, units = ffn_in.shape
    wg_flat = qkv_global_weight.reshape(-1)
    fi_flat = ffn_in.reshape(-1)
    fo_flat = ffn_out.reshape(-1)
    n_wg, n_fi = (wg_flat.shape[0], fi_flat.shape[0])
    everything = lax.all_gather(jnp.concatenate([wg_flat, fi_flat, fo_flat]), "row", axis=0)
    w_global = everything[:, :n_wg].reshape(n_row * wg_rows, heads_here * triple)
    f_in = everything[:, n_wg : n_wg + n_fi].reshape(n_row * fi_rows, units)
    f_out = jnp.transpose(
        everything[:, n_wg + n_fi :].reshape(n_row, units, ffn_out.shape[1]), (1, 0, 2)
    ).reshape(units, n_row * ffn_out.shape[1])
    w_out = lax.all_gather(out_weight, "col", axis=0, tiled=True)
    flat_weight = qkv_weight.reshape(width, heads_here * triple)
    qkv = jnp.dot(tokens, flat_weight, preferred_element_type=jnp.float32).astype(jnp.bfloat16)
    qkv_heads = qkv.reshape(shard_len, heads_here, triple)
    queries = qkv_heads[:, :, :head_dim]
    kv_local = qkv_heads[:, :, head_dim:]
    owners = page_owner[0, :, 0]
    n_pages = owners.shape[0]
    page_len = shard_len // n_pages
    capacity = max(2, n_pages // n_seq)
    page_order = jnp.arange(n_pages, dtype=jnp.int32)
    slot = jnp.sum(
        ((owners[:, None] == owners[None, :]) & (page_order[None, :] < page_order[:, None])).astype(
            jnp.int32
        ),
        axis=1,
    )
    target = owners * capacity + slot
    placing = (target[None, :] == jnp.arange(n_seq * capacity, dtype=jnp.int32)[:, None]).astype(
        jnp.bfloat16
    )
    outgoing = jnp.dot(
        placing,
        kv_local.reshape(n_pages, page_len * heads_here * 2 * head_dim),
        preferred_element_type=jnp.float32,
    ).astype(jnp.bfloat16)
    outgoing = outgoing.reshape(n_seq, capacity, page_len, heads_here, 2 * head_dim)
    arrived = lax.all_to_all(outgoing, "seq", split_axis=0, concat_axis=0, tiled=True)
    page_pool = arrived[None, None]
    kv_ext = padded(kv_local, (("seq", 0),), HALF)
    glob_qkv = jnp.dot(glob_rows, flat_weight, preferred_element_type=jnp.float32).astype(
        jnp.bfloat16
    )
    glob_kv = glob_qkv.reshape(n_glob, heads_here, triple)[:, :, head_dim:]
    glob_k = glob_kv[:, :, :head_dim]
    glob_v = glob_kv[:, :, head_dim:]
    glob_q = (
        jnp.dot(glob_rows, w_global, preferred_element_type=jnp.float32)
        .astype(jnp.bfloat16)
        .reshape(n_glob, heads_here, triple)[:, :, :head_dim]
    )
    global_kv_local = (
        jnp.dot(tokens, w_global, preferred_element_type=jnp.float32)
        .astype(jnp.bfloat16)
        .reshape(shard_len, heads_here, triple)[:, :, head_dim:]
    )
    seg_all = segment_ids[0]
    glob_seg = jnp.take(seg_all, all_pos)
    seg_pad = jnp.pad(seg_all, (HALF, HALF), constant_values=-1)
    query_seg = lax.dynamic_slice_in_dim(seg_all, base, shard_len, 0)
    key_seg = lax.dynamic_slice_in_dim(seg_pad, base, shard_len + 2 * HALF, 0)
    key_pos = base - HALF + jnp.arange(shard_len + 2 * HALF, dtype=jnp.int32)
    key_flag = jnp.any(key_pos[:, None] == all_pos[None, :], axis=1)
    query_pos = base + local_order
    s_part = (
        jnp.einsum(
            "ghd,khd->hgk",
            glob_q,
            global_kv_local[:, :, :head_dim],
            preferred_element_type=jnp.float32,
        )
        * scale
    )
    part_mask = glob_seg[:, None] == query_seg[None, :]
    part_top = jnp.max(jnp.where(part_mask, s_part, neg), axis=2)
    glob_top = lax.pmax(part_top, "seq")
    e_part = jnp.where(part_mask, jnp.exp(s_part - glob_top[:, :, None]), 0.0)
    part_total = jnp.sum(e_part, axis=2)
    part_acc = jnp.einsum(
        "hgk,khd->hgd",
        e_part,
        global_kv_local[:, :, head_dim:].astype(jnp.float32),
        precision=lax.Precision.HIGHEST,
    )
    summed = lax.psum(jnp.concatenate([part_acc, part_total[:, :, None]], axis=2), "seq")
    glob_out = (summed[:, :, :head_dim] / summed[:, :, head_dim:]).astype(jnp.bfloat16)
    glob_mask = query_seg[:, None] == glob_seg[None, :]
    k_blk = kv_ext[:, :, :head_dim]
    v_blk = kv_ext[:, :, head_dim:]
    s_win = jnp.einsum("qhd,khd->hqk", queries, k_blk, preferred_element_type=jnp.float32) * scale
    s_glob = jnp.einsum("qhd,ghd->hqg", queries, glob_k, preferred_element_type=jnp.float32) * scale
    m_win = (
        (jnp.abs(query_pos[:, None] - key_pos[None, :]) <= HALF)
        & (query_seg[:, None] == key_seg[None, :])
        & jnp.logical_not(key_flag[None, :])
    )
    top = jnp.maximum(
        jnp.max(jnp.where(m_win, s_win, neg), axis=2),
        jnp.max(jnp.where(glob_mask, s_glob, neg), axis=2),
    )
    e_win = jnp.where(m_win, jnp.exp(s_win - top[:, :, None]), 0.0)
    e_glob = jnp.where(glob_mask, jnp.exp(s_glob - top[:, :, None]), 0.0)
    total = jnp.sum(e_win, axis=2) + jnp.sum(e_glob, axis=2)
    numer = jnp.einsum(
        "hqk,khd->qhd", e_win.astype(jnp.bfloat16), v_blk, preferred_element_type=jnp.float32
    )
    numer = numer + jnp.einsum(
        "hqg,ghd->qhd", e_glob.astype(jnp.bfloat16), glob_v, preferred_element_type=jnp.float32
    )
    pieces = (numer / jnp.transpose(total)[:, :, None]).astype(jnp.bfloat16)
    own_out = lax.dynamic_slice_in_dim(glob_out, seq_index * per_shard, per_shard, 1)
    placed = jnp.einsum("gt,hgd->thd", picker, own_out, preferred_element_type=jnp.float32).astype(
        jnp.bfloat16
    )
    is_own = jnp.any(own_match, axis=0)
    attention = jnp.where(is_own[:, None, None], placed, pieces).reshape(
        shard_len, heads_here * head_dim
    )
    attn_all = lax.all_gather(attention, "col", axis=0)
    attn_full = jnp.transpose(attn_all, (1, 0, 2)).reshape(shard_len, n_col * heads_here * head_dim)
    proj = jnp.dot(attn_full, w_out, preferred_element_type=jnp.float32)
    middle = layer_norm(tokens.astype(jnp.float32) + proj, ln_gain, ln_bias).astype(jnp.bfloat16)
    ffn_pre = jnp.dot(middle, f_in, preferred_element_type=jnp.float32)
    ffn_hidden = jax.nn.gelu(ffn_pre, approximate=False).astype(jnp.bfloat16)
    ffn_part = lax.psum_scatter(
        jnp.dot(ffn_hidden, f_out, preferred_element_type=jnp.float32),
        "col",
        scatter_dimension=0,
        tiled=True,
    )
    out_rows = shard_len // n_col
    mine = lax.dynamic_slice_in_dim(middle, col_index * out_rows, out_rows, 0).astype(jnp.float32)
    normed = layer_norm(mine + ffn_part, ln2_gain, ln2_bias)
    return (normed.astype(jnp.bfloat16)[None], page_pool)


def solution(mesh):
    in_specs = (
        P("row", "seq", None),
        P(None, "col", None),
        P("row", "col", None),
        P("col", None),
        P(),
        P(),
        P("row", "col"),
        P("col", "row"),
        P(),
        P(),
        P("row", None),
        P("row", None),
        P("row", "seq", None),
    )
    out_specs = (P("row", ("seq", "col"), None), P("row", "seq", None, None, None, "col", None))
    return jax.shard_map(
        per_device, mesh=mesh, in_specs=in_specs, out_specs=out_specs, check_vma=False
    )
```

profile of v0, /device:TPU:1, one launch (start us, length us, event | category | flops | bytes accessed | tf_op | source)
XLA Modules:
  0.0 554.5 jit_solution(4400960408158859480)
XLA Ops:
  7.2 1.4 copy.58
  8.7 1.5 reshape.172
  10.3 0.4 copy.71
  10.8 0.5 copy-done.11
  11.2 1.2 pad_maximum_fusion
  12.5 0.4 copy-done.6
  12.9 1.9 convolution_convert_fusion.1
  14.9 1.4 copy.61
  16.3 0.8 fusion.140
  17.1 5.4 collective-permute-start
  22.5 5.4 collective-permute-start.1
  28.3 32.6 %all-gather.1 = bf16[32,4,1024]{2,1,0:T(4,128)(2,1)S(1)} all-gather(bf16[1,4,1024]{2,1,0:T(4,128)(2,1)S(1)} %fusion.24), channel_id=1, replica_groups=mesh['seq'=32,'row'=4,'col'=4] {'seq'}, dimensions={0}, use_global_device_ids=true | all-gather | bytes 270336 | tf_op jit(solution)/shard_map/all_gather | solution.py:65
  61.0 1.1 gather_fusion
  62.2 0.4 compare_reduce_fusion
  62.9 0.8 fusion.15
  63.8 0.7 convolution_convert_fusion.4
  64.6 0.9 copy.62
  65.4 1.2 select_reduce_fusion.1
  66.7 1.2 pad_maximum_fusion.1
  67.9 1.7 select_reduce_fusion
  69.9 2.7 fusion
  72.8 2.0 fusion.70
  74.8 9.9 %all-gather.10.cloned.1.call-done = bf16[2883584]{0:T(1024)(128)(2,1)} async-done(((bf16[720896]{0:T(1024)(128)(2,1)}), bf16[2883584]{0:T(1024)(128)(2,1)}) %all-gather.10.cloned.1.call-update) | async-done | bytes 5767184 | tf_op jit(solution)/shard_map/all_gather | solution.py:72
  84.7 7.2 %reshape.195 = bf16[4,720896]{1,0:T(4,128)(2,1)} reshape(bf16[2883584]{0:T(1024)(128)(2,1)} %all-gather.10.cloned.1.call-done) | data formatting | bytes 11534336 | tf_op jit(solution)/shard_map/all_gather | solution.py:72
  91.9 1.4 slice-done
  93.3 1.4 reshape.175
  94.7 0.4 convolution_convert_fusion.5
  95.1 3.2 convolution_convert_fusion.2
  98.5 1.5 select_reduce_fusion.2
  100.0 53.4 %pmax.7 = f32[4,128]{1,0:T(4,128)S(1)} all-reduce(f32[4,128]{1,0:T(4,128)S(1)} %get-tuple-element.10), channel_id=1, replica_groups=mesh['seq'=32,'row'=4,'col'=4] {'seq'}, use_global_device_ids=true, to_apply=%region_2.3 | all-reduce | flops 512 | bytes 4096 | tf_op jit(solution)/shard_map/pmax | solution.py:143
  153.5 1.9 fusion.67
  155.4 0.4 fusion.66
  155.7 0.7 pad_maximum_fusion.2
  156.5 5.3 fusion.63
  161.8 205.0 %all-reduce.3.cloned.1.call-done = f32[4,128,65]{1,2,0:T(8,128)} async-done(((f32[4,128,65]{1,2,0:T(8,128)}), f32[4,128,65]{1,2,0:T(8,128)}) %all-reduce.3.cloned.1.call-update) | async-done | bytes 133136 | tf_op jit(solution)/shard_map/psum | solution.py:152
  366.8 0.7 slice.79
  367.6 0.9 slice.78
  368.8 0.8 copy.64
  369.7 0.5 all-gather.8.cloned.1.call-update
  370.3 4.0 fusion.139
  374.3 1.6 copy.74
  375.9 4.0 copy.66
  379.9 4.8 reshape.182
  384.7 23.1 %all-gather.6.cloned.1.call-done = bf16[4,512,256]{2,1,0:T(8,128)(2,1)} async-done(((bf16[1,512,256]{2,1,0:T(8,128)(2,1)}), bf16[4,512,256]{2,1,0:T(8,128)(2,1)}) %all-gather.6.cloned.1.call-update) | async-done | bytes 1048592 | tf_op jit(solution)/shard_map/all_gather | solution.py:186
  407.8 1.7 copy.65
  409.5 53.6 %all-gather.8.cloned.1.call-done = bf16[1024,1024]{1,0:T(8,128)(2,1)} async-done(((bf16[256,1024]{1,0:T(8,128)(2,1)}), bf16[1024,1024]{1,0:T(8,128)(2,1)}) %all-gather.8.cloned.1.call-update) | async-done | bytes 2097168 | tf_op jit(solution)/shard_map/all_gather | solution.py:78
  463.1 2.9 fusion.141
  466.1 0.3 multiply_reduce_fusion
  466.4 0.3 copy-done.17
  466.7 0.4 add_convert_fusion
  467.2 1.0 copy-done.8
  468.1 9.8 %fusion.25 = f32[512,1024]{1,0:T(8,128)} fusion(bf16[1024,1024]{0,1:T(8,128)(2,1)} %bitcast.92, bf16[512,1024]{1,0:T(8,128)(2,1)S(1)} %add_convert_fusion, bf16[1024,1024]{1,0:T(8,128)(2,1)} %reshape.182), kind=kOutput, calls=%fused_computation.47 | convolution fusion | flops 2181562368 | bytes 7340032 | tf_op jit(solution)/shard_map/dot_general | solution.py:193
  477.9 1.0 copy-done.5
  479.0 0.3 copy.67
  479.3 0.4 reshape.185
  479.9 0.4 convolution_convert_fusion
  480.3 1.6 reshape.186
  481.9 9.3 %all-to-all-start = ((bf16[32,2,16,4,128]{4,3,2,1,0:T(4,128)(2,1)}), bf16[32,2,16,4,128]{4,3,2,1,0:T(4,128)(2,1)S(1)}, u32[]{:S(2)}, u32[]{:S(2)}) async-start(bf16[32,2,16,4,128]{4,3,2,1,0:T(4,128)(2,1)} %reshape.186), calls=%async_computation.1 | async-start | bytes 2097152 | tf_op jit(solution)/shard_map/all_to_all | solution.py:105
  491.1 28.1 %all-to-all-done = bf16[32,2,16,4,128]{4,3,2,1,0:T(4,128)(2,1)S(1)} async-done(((bf16[32,2,16,4,128]{4,3,2,1,0:T(4,128)(2,1)}), bf16[32,2,16,4,128]{4,3,2,1,0:T(4,128)(2,1)S(1)}, u32[]{:S(2)}, u32[]{:S(2)}) %all-to-all-start) | async-done | bytes 1048608 | tf_op jit(solution)/shard_map/all_to_all | solution.py:105
  519.3 23.1 %reduce-scatter.2.cloned.1.call-done = f32[128,1024]{1,0:T(8,128)} async-done(((f32[512,1024]{1,0:T(8,128)}), f32[128,1024]{1,0:T(8,128)}) %reduce-scatter.2.cloned.1.call-update) | async-done | bytes 524304 | tf_op jit(solution)/shard_map/reduce_scatter | solution.py:192
  542.3 1.4 fusion.86
  543.7 1.3 multiply_reduce_fusion.1
  545.0 2.0 fusion.81
  547.0 1.0 copy.77
  (81 shorter events, 2.6 us)
Async XLA Ops:
  7.2 5.3 copy-start
  7.2 3.1 copy-start.14
  7.2 3.1 copy-start.15
  7.2 77.5 %all-gather.10.cloned.1.call-start = ((), (), s32[]{:S(2)}) async-start(), calls=%async_computation.6 | async-start | bytes 7208960 | tf_op jit(solution)/shard_map/all_gather | solution.py:72
  10.2 1.0 copy-start.11
  11.2 1.7 copy-start.6
  12.4 354.4 %all-reduce.3.cloned.1.call-start = ((), (), s32[]{:S(2)}) async-start(), calls=%async_computation.2 | async-start | bytes 294912 | tf_op jit(solution)/shard_map/psum | solution.py:152
  14.8 13.1 %copy-start.21 = (s32[1,128]{1,0:T(1,128)S(1)}, s32[1,128]{1,0:T(1,128)}, u32[]{:S(2)}) copy-start(s32[1,128]{1,0:T(1,128)} %param.24) | copy-start | bytes 1540
  14.9 46.1 %copy-start.3 = (s32[1,16384]{1,0:T(1,128)S(1)}, s32[1,16384]{1,0:T(1,128)}, u32[]{:S(2)}) copy-start(s32[1,16384]{1,0:T(1,128)} %param.23) | copy-start | bytes 196612
  17.1 49.5 %collective-permute-start = (bf16[256,4,128]{0,2,1:T(8,128)(2,1)}, bf16[256,4,128]{0,2,1:T(8,128)(2,1)}, u32[]{:S(2)}, u32[]{:S(2)}) collective-permute-start(bf16[256,4,128]{0,2,1:T(8,128)(2,1)} %get-tuple-element.4), channel_id=1, source_target_pairs={{0,16},{16,32},{32,48},{48,64},{64,80},{80,96},{96,112},{112,128},... | collective-permute-start | bytes 786440 | tf_op jit(solution)/shard_map/ppermute | solution.py:15
  22.5 44.2 %collective-permute-start.1 = (bf16[256,4,128]{0,2,1:T(8,128)(2,1)}, bf16[256,4,128]{0,2,1:T(8,128)(2,1)}, u32[]{:S(2)}, u32[]{:S(2)}) collective-permute-start(bf16[256,4,128]{0,2,1:T(8,128)(2,1)} %get-tuple-element.5), channel_id=1, source_target_pairs={{16,0},{32,16},{48,32},{64,48},{80,64},{96,80},{112,96},{128,112},... | collective-permute-start | bytes 786440 | tf_op jit(solution)/shard_map/ppermute | solution.py:18
  63.7 6.1 %copy-start.9 = (pred[512,1024]{1,0:T(8,128)(4,1)}, pred[512,1024]{1,0:T(8,128)(4,1)S(1)}, u32[]{:S(2)}) copy-start(pred[512,1024]{1,0:T(8,128)(4,1)S(1)} %fusion.15) | copy-start | bytes 1572868
  64.5 5.0 copy-start.4
  67.9 1.7 copy-start.12
  69.6 3.2 copy-start.2
  91.9 1.4 slice-start
  98.5 58.0 %copy-start.10 = (pred[512,1024]{1,0:T(8,128)(4,1)S(1)}, pred[512,1024]{1,0:T(8,128)(4,1)}, u32[]{:S(2)}) copy-start(pred[512,1024]{1,0:T(8,128)(4,1)} %copy-done.9) | copy-start | bytes 1572868
  98.5 58.0 %copy-start.13 = (bf16[1024,4,128]{0,2,1:T(8,128)(2,1)S(1)}, bf16[1024,4,128]{0,2,1:T(8,128)(2,1)}, u32[]{:S(2)}) copy-start(bf16[1024,4,128]{0,2,1:T(8,128)(2,1)} %copy-done.12) | copy-start | bytes 3145732
  98.5 58.0 %copy-start.16 = (f32[4,64,512]{2,1,0:T(8,128)S(1)}, f32[4,64,512]{2,1,0:T(8,128)}, u32[]{:S(2)}) copy-start(f32[4,64,512]{2,1,0:T(8,128)} %fusion.70) | copy-start | bytes 1572868
  156.4 251.3 %all-gather.6.cloned.1.call-start = ((), (), s32[]{:S(2)}) async-start(), calls=%async_computation.3 | async-start | bytes 1310720 | tf_op jit(solution)/shard_map/all_gather | solution.py:186
  369.7 93.4 %all-gather.8.cloned.1.call-start = ((), (), s32[]{:S(2)}) async-start(), calls=%async_computation.4 | async-start | bytes 2621440 | tf_op jit(solution)/shard_map/all_gather | solution.py:78
  370.3 172.1 %reduce-scatter.2.cloned.1.call-start = ((), (), s32[]{:S(2)}) async-start(), calls=%async_computation.5 | async-start | bytes 2621440 | tf_op jit(solution)/shard_map/reduce_scatter | solution.py:192
  384.7 78.4 %copy-start.7 = (bf16[1,512,1024]{2,1,0:T(8,128)(2,1)S(1)}, bf16[1,512,1024]{2,1,0:T(8,128)(2,1)}, u32[]{:S(2)}) copy-start(bf16[1,512,1024]{2,1,0:T(8,128)(2,1)} %param.13) | copy-start | bytes 3145732
  466.0 0.7 copy-start.17
  466.0 0.7 copy-start.18
  467.2 1.0 copy-start.8
  477.9 1.0 copy-start.5
  477.9 1.8 copy-start.22
  481.8 63.2 %copy-start.19 = (f32[1024]{0:T(1024)S(1)}, f32[1024]{0:T(1024)}, u32[]{:S(2)}) copy-start(f32[1024]{0:T(1024)} %param.22) | copy-start | bytes 12292
  481.9 63.2 %copy-start.20 = (f32[1024]{0:T(1024)S(1)}, f32[1024]{0:T(1024)}, u32[]{:S(2)}) copy-start(f32[1024]{0:T(1024)} %param.21) | copy-start | bytes 12292
  481.9 37.4 %all-to-all-start = ((bf16[32,2,16,4,128]{4,3,2,1,0:T(4,128)(2,1)}), bf16[32,2,16,4,128]{4,3,2,1,0:T(4,128)(2,1)S(1)}, u32[]{:S(2)}, u32[]{:S(2)}) async-start(bf16[32,2,16,4,128]{4,3,2,1,0:T(4,128)(2,1)} %reshape.186), calls=%async_computation.1 | async-start | bytes 2097152 | tf_op jit(solution)/shard_map/all_to_all | solution.py:105
  542.3 5.7 %copy-start.1 = (bf16[1024,4,192]{0,2,1:T(8,128)(2,1)S(1)}, bf16[1024,4,192]{0,2,1:T(8,128)(2,1)}, u32[]{:S(2)}) copy-start(bf16[1024,4,192]{0,2,1:T(8,128)(2,1)} %param.14) | copy-start | bytes 4718596
Sparse Core Ops, SparseCore 0:
  12.6 72.0 all-gather.9
  156.6 210.2 all-reduce.2
  369.8 37.9 all-gather.5
  409.9 53.1 all-gather.7
  478.1 64.2 reduce-scatter.1
where the time goes:
time: 556 us; the launch traced here: 555 us
  waiting for transfers between devices  343 us (62%)
  blocking collectives  86.1 us (15%)
  local copies, waits for them, and re-layouts  43.5 us (8%)
  matrix products  33.5 us (6%)
  starting transfers between devices  20.2 us (4%)
  between operations  14.3 us (3%)
  other arithmetic  13.6 us (2%)
    psum x1, waiting for transfers between devices, per_device(): lax.psum(jnp.concatenate([part_acc, part_total[:, :, None]], axis=2), 'seq')  205 us
    all_gather x1, waiting for transfers between devices, per_device(): w_out = lax.all_gather(out_weight, 'col', axis=0, tiled=True)  53.6 us
    pmax x1, blocking collectives, per_device(): glob_top = lax.pmax(part_top, 'seq')  53.4 us
    all_gather x1, blocking collectives, per_device(): glob_rows = lax.all_gather(own_rows, 'seq', axis=0, tiled=True)  32.6 us
    all_to_all x1, waiting for transfers between devices, per_device(): lax.all_to_all(outgoing, 'seq', split_axis=0, concat_axis=0, tiled=True)  28.1 us
    reduce_scatter x1, waiting for transfers between devices, per_device(): lax.psum_scatter(jnp.dot(ffn_hidden, f_out, preferred_element_type=jnp.fl...  23.1 us
    all_gather x1, waiting for transfers between devices, per_device(): attn_all = lax.all_gather(attention, 'col', axis=0)  23.1 us
  transfers between devices with their start and end apart: 8, of which 6 were waited for; matrix products, arithmetic and copies ran while one was open for 8% of the time, Pallas kernels for 0%

commit v1 on v0

--- a/solution.py
+++ b/solution.py
@@ -149,7 +149,9 @@
         global_kv_local[:, :, head_dim:].astype(jnp.float32),
         precision=lax.Precision.HIGHEST,
     )
-    summed = lax.psum(jnp.concatenate([part_acc, part_total[:, :, None]], axis=2), "seq")
+    block_2 = jnp.concatenate([part_acc, part_total[:, :, None]], axis=2)
+    terms = lax.all_gather(block_2, "seq", axis=0, tiled=False)
+    summed = terms.sum(axis=0)
     glob_out = (summed[:, :, :head_dim] / summed[:, :, head_dim:]).astype(jnp.bfloat16)
     glob_mask = query_seg[:, None] == glob_seg[None, :]
     k_blk = kv_ext[:, :, :head_dim]

time: 556 us -> 415 us (0.75)
  waiting for transfers between devices: 343 us -> 206 us
    psum x1 -> x0, waiting for transfers between devices: 205 us -> none  [per_device(): lax.psum(jnp.concatenate([part_acc, part_total[:, :, None]], axis=2), 'seq')]
    all_gather x0 -> x1, waiting for transfers between devices: none -> 48.6 us  [per_device(): terms = lax.all_gather(block_2, 'seq', axis=0, tiled=False)]
    all_gather x1, waiting for transfers between devices: 9.93 us -> 32.3 us  [per_device(): lax.all_gather(jnp.concatenate([wg_flat, fi_flat, fo_flat]), 'row', axis=0)]
  transfers between devices with their start and end apart: 8 -> 8, of which waited for: 6 -> 7; matrix products, arithmetic and copies ran while one was open for 8% -> 9% of each run, Pallas kernels for 0% -> 0%
where the time goes in v1:
time: 415 us; the launch traced here: 414 us
  waiting for transfers between devices  206 us (50%)
  blocking collectives  91 us (22%)
  local copies, waits for them, and re-layouts  39 us (9%)
  matrix products  30 us (7%)
  starting transfers between devices  17.4 us (4%)
  other arithmetic  16.2 us (4%)
  between operations  14.2 us (3%)
    all_gather x1, waiting for transfers between devices, per_device(): w_out = lax.all_gather(out_weight, 'col', axis=0, tiled=True)  53.4 us
    pmax x1, blocking collectives, per_device(): glob_top = lax.pmax(part_top, 'seq')  53.2 us
    all_gather x1, waiting for transfers between devices, per_device(): terms = lax.all_gather(block_2, 'seq', axis=0, tiled=False)  48.6 us
    all_gather x1, blocking collectives, per_device(): glob_rows = lax.all_gather(own_rows, 'seq', axis=0, tiled=True)  37.8 us
    all_gather x1, waiting for transfers between devices, per_device(): lax.all_gather(jnp.concatenate([wg_flat, fi_flat, fo_flat]), 'row', axis=0)  32.3 us
    all_to_all x1, waiting for transfers between devices, per_device(): lax.all_to_all(outgoing, 'seq', split_axis=0, concat_axis=0, tiled=True)  28.3 us
    reduce_scatter x1, waiting for transfers between devices, per_device(): lax.psum_scatter(jnp.dot(ffn_hidden, f_out, preferred_element_type=jnp.fl...  22.1 us
    all_gather x1, waiting for transfers between devices, per_device(): attn_all = lax.all_gather(attention, 'col', axis=0)  20.8 us
  transfers between devices with their start and end apart: 8, of which 7 were waited for; matrix products, arithmetic and copies ran while one was open for 9% of the time, Pallas kernels for 0%

profile of v1, /device:TPU:1, one launch (start us, length us, event | category | flops | bytes accessed | tf_op | source)
XLA Modules:
  0.0 414.1 jit_solution(10061713030474531043)
XLA Ops:
  7.2 1.4 copy.55
  8.7 0.8 reshape.172
  9.6 0.4 copy.69
  10.0 1.2 pad_maximum_fusion
  11.4 0.3 copy-done.4
  11.8 0.3 fusion.24
  12.0 37.8 %all-gather.2 = bf16[32,4,1024]{2,1,0:T(4,128)(2,1)S(1)} all-gather(bf16[1,4,1024]{2,1,0:T(4,128)(2,1)S(1)} %fusion.24), channel_id=1, replica_groups=mesh['seq'=32,'row'=4,'col'=4] {'seq'}, dimensions={0}, use_global_device_ids=true | all-gather | bytes 270336 | tf_op jit(solution)/shard_map/all_gather | solution.py:65
  49.9 1.1 gather_fusion
  51.2 32.3 %all-gather.12.cloned.1.call-done = bf16[2883584]{0:T(1024)(128)(2,1)} async-done(((bf16[720896]{0:T(1024)(128)(2,1)}), bf16[2883584]{0:T(1024)(128)(2,1)}) %all-gather.12.cloned.1.call-update) | async-done | bytes 5767184 | tf_op jit(solution)/shard_map/all_gather | solution.py:72
  83.6 7.2 %reshape.195 = bf16[4,720896]{1,0:T(4,128)(2,1)} reshape(bf16[2883584]{0:T(1024)(128)(2,1)} %all-gather.12.cloned.1.call-done) | data formatting | bytes 11534336 | tf_op jit(solution)/shard_map/all_gather | solution.py:72
  90.8 1.4 slice-done
  92.2 2.6 reshape.175
  94.8 3.7 convolution_convert_fusion.2
  98.5 0.4 convolution_convert_fusion.5
  99.1 2.4 select_reduce_fusion.2
  101.5 53.2 %pmax.7 = f32[4,128]{1,0:T(4,128)S(1)} all-reduce(f32[4,128]{1,0:T(4,128)S(1)} %get-tuple-element.10), channel_id=1, replica_groups=mesh['seq'=32,'row'=4,'col'=4] {'seq'}, use_global_device_ids=true, to_apply=%region_2.3 | all-reduce | flops 512 | bytes 4096 | tf_op jit(solution)/shard_map/pmax | solution.py:143
  154.7 2.3 fusion.67
  157.0 0.3 fusion.66
  157.4 0.7 pad_maximum_fusion.2
  158.1 1.9 convolution_convert_fusion.1
  160.0 1.4 copy.58
  161.5 0.8 fusion.137
  162.3 3.0 collective-permute-start
  165.3 4.9 %collective-permute-start.1 = (bf16[256,4,128]{0,2,1:T(8,128)(2,1)}, bf16[256,4,128]{0,2,1:T(8,128)(2,1)}, u32[]{:S(2)}, u32[]{:S(2)}) collective-permute-start(bf16[256,4,128]{0,2,1:T(8,128)(2,1)} %get-tuple-element.5), channel_id=1, source_target_pairs={{16,0},{32,16},{48,32},{64,48},{80,64},{96,80},{112,96},{128,112},... | collective-permute-start | bytes 786440 | tf_op jit(solution)/shard_map/ppermute | solution.py:18
  170.3 0.4 compare_reduce_fusion
  170.8 0.8 fusion.15
  171.6 0.7 convolution_convert_fusion.4
  172.6 0.4 select_reduce_fusion.1
  173.0 0.3 collective-permute-done.1
  173.3 1.2 pad_maximum_fusion.1
  174.4 1.7 select_reduce_fusion
  176.1 0.2 fusion.68
  176.4 2.7 fusion
  179.1 0.3 fusion.70
  179.4 2.1 fusion.63
  181.5 48.6 %all-gather.14.cloned.1.call-done = f32[128,128,65]{1,2,0:T(8,128)} async-done(((f32[4,128,65]{1,2,0:T(8,128)}), f32[128,128,65]{1,2,0:T(8,128)}) %all-gather.14.cloned.1.call-update) | async-done | bytes 4259856 | tf_op jit(solution)/shard_map/all_gather | solution.py:153
  230.1 2.6 reduce_sum.82
  232.9 0.4 fusion.23
  233.3 0.8 copy.61
  234.2 0.5 all-gather.10.cloned.1.call-update
  234.8 4.0 fusion.136
  238.8 1.6 copy.72
  240.4 4.0 copy.63
  244.4 4.8 %reshape.182 = bf16[1024,1024]{1,0:T(8,128)(2,1)} reshape(bf16[4,262144]{1,0:T(4,128)(2,1)} %get-tuple-element.2) | data formatting | bytes 4194304 | tf_op jit(solution)/shard_map/reshape | solution.py:74
  249.2 20.8 %all-gather.8.cloned.1.call-done = bf16[4,512,256]{2,1,0:T(8,128)(2,1)} async-done(((bf16[1,512,256]{2,1,0:T(8,128)(2,1)}), bf16[4,512,256]{2,1,0:T(8,128)(2,1)}) %all-gather.8.cloned.1.call-update) | async-done | bytes 1048592 | tf_op jit(solution)/shard_map/all_gather | solution.py:188
  270.0 1.7 copy.62
  271.7 53.4 %all-gather.10.cloned.1.call-done = bf16[1024,1024]{1,0:T(8,128)(2,1)} async-done(((bf16[256,1024]{1,0:T(8,128)(2,1)}), bf16[1024,1024]{1,0:T(8,128)(2,1)}) %all-gather.10.cloned.1.call-update) | async-done | bytes 2097168 | tf_op jit(solution)/shard_map/all_gather | solution.py:78
  325.1 2.9 fusion.138
  328.1 0.3 multiply_reduce_fusion
  328.4 0.3 copy-done.11
  328.7 0.4 add_convert_fusion
  329.2 10.2 %fusion.25 = f32[512,1024]{1,0:T(8,128)} fusion(bf16[1024,1024]{0,1:T(8,128)(2,1)} %bitcast.94, bf16[512,1024]{1,0:T(8,128)(2,1)S(1)} %add_convert_fusion, bf16[1024,1024]{1,0:T(8,128)(2,1)} %reshape.182), kind=kOutput, calls=%fused_computation.47 | convolution fusion | flops 2181562368 | bytes 7340032 | tf_op jit(solution)/shard_map/dot_general | solution.py:195
  339.3 0.3 copy.64
  339.7 0.4 reshape.185
  340.1 0.2 convert_reduce_fusion
  340.3 0.4 convolution_convert_fusion
  340.7 1.6 reshape.186
  342.2 9.3 %all-to-all-start = ((bf16[32,2,16,4,128]{4,3,2,1,0:T(4,128)(2,1)}), bf16[32,2,16,4,128]{4,3,2,1,0:T(4,128)(2,1)S(1)}, u32[]{:S(2)}, u32[]{:S(2)}) async-start(bf16[32,2,16,4,128]{4,3,2,1,0:T(4,128)(2,1)} %reshape.186), calls=%async_computation.1 | async-start | bytes 2097152 | tf_op jit(solution)/shard_map/all_to_all | solution.py:105
  351.5 28.3 %all-to-all-done = bf16[32,2,16,4,128]{4,3,2,1,0:T(4,128)(2,1)S(1)} async-done(((bf16[32,2,16,4,128]{4,3,2,1,0:T(4,128)(2,1)}), bf16[32,2,16,4,128]{4,3,2,1,0:T(4,128)(2,1)S(1)}, u32[]{:S(2)}, u32[]{:S(2)}) %all-to-all-start) | async-done | bytes 1048608 | tf_op jit(solution)/shard_map/all_to_all | solution.py:105
  379.8 22.1 %reduce-scatter.2.cloned.1.call-done = f32[128,1024]{1,0:T(8,128)} async-done(((f32[512,1024]{1,0:T(8,128)}), f32[128,1024]{1,0:T(8,128)}) %reduce-scatter.2.cloned.1.call-update) | async-done | bytes 524304 | tf_op jit(solution)/shard_map/reduce_scatter | solution.py:194
  402.0 1.4 fusion.86
  403.3 1.3 multiply_reduce_fusion.1
  404.7 2.0 fusion.81
  406.6 1.0 copy.74
  (72 shorter events, 1.7 us)
Async XLA Ops:
  7.2 151.0 %copy-start = (bf16[1024,4,192]{0,2,1:T(8,128)(2,1)S(1)}, bf16[1024,4,192]{0,2,1:T(8,128)(2,1)}, u32[]{:S(2)}) copy-start(bf16[1024,4,192]{0,2,1:T(8,128)(2,1)} %param.14) | copy-start | bytes 4718596
  7.2 2.3 copy-start.9
  7.2 2.4 copy-start.10
  7.2 76.4 %all-gather.12.cloned.1.call-start = ((), (), s32[]{:S(2)}) async-start(), calls=%async_computation.5 | async-start | bytes 7208960 | tf_op jit(solution)/shard_map/all_gather | solution.py:72
  10.0 1.3 copy-start.15
  10.0 1.7 copy-start.4
  11.3 38.7 %copy-start.3 = (s32[1,16384]{1,0:T(1,128)S(1)}, s32[1,16384]{1,0:T(1,128)}, u32[]{:S(2)}) copy-start(s32[1,16384]{1,0:T(1,128)} %param.23) | copy-start | bytes 196612
  11.3 218.8 %all-gather.14.cloned.1.call-start = ((), (), s32[]{:S(2)}) async-start(), calls=%async_computation.6 | async-start | bytes 4866048 | tf_op jit(solution)/shard_map/all_gather | solution.py:153
  90.8 1.4 slice-start
  94.8 3.7 copy-start.2
  99.1 59.0 %copy-start.5 = (bf16[1,512,1024]{2,1,0:T(8,128)(2,1)S(1)}, bf16[1,512,1024]{2,1,0:T(8,128)(2,1)}, u32[]{:S(2)}) copy-start(bf16[1,512,1024]{2,1,0:T(8,128)(2,1)} %param.13) | copy-start | bytes 3145732
  154.7 2.3 copy-start.8
  158.1 111.9 %all-gather.8.cloned.1.call-start = ((), (), s32[]{:S(2)}) async-start(), calls=%async_computation.2 | async-start | bytes 1310720 | tf_op jit(solution)/shard_map/all_gather | solution.py:188
  162.3 10.7 %collective-permute-start = (bf16[256,4,128]{0,2,1:T(8,128)(2,1)}, bf16[256,4,128]{0,2,1:T(8,128)(2,1)}, u32[]{:S(2)}, u32[]{:S(2)}) collective-permute-start(bf16[256,4,128]{0,2,1:T(8,128)(2,1)} %get-tuple-element.4), channel_id=1, source_target_pairs={{0,16},{16,32},{32,48},{48,64},{64,80},{80,96},{96,112},{112,128},... | collective-permute-start | bytes 786440 | tf_op jit(solution)/shard_map/ppermute | solution.py:15
  165.3 8.0 %collective-permute-start.1 = (bf16[256,4,128]{0,2,1:T(8,128)(2,1)}, bf16[256,4,128]{0,2,1:T(8,128)(2,1)}, u32[]{:S(2)}, u32[]{:S(2)}) collective-permute-start(bf16[256,4,128]{0,2,1:T(8,128)(2,1)} %get-tuple-element.5), channel_id=1, source_target_pairs={{16,0},{32,16},{48,32},{64,48},{80,64},{96,80},{112,96},{128,112},... | collective-permute-start | bytes 786440 | tf_op jit(solution)/shard_map/ppermute | solution.py:18
  234.2 90.9 %all-gather.10.cloned.1.call-start = ((), (), s32[]{:S(2)}) async-start(), calls=%async_computation.3 | async-start | bytes 2621440 | tf_op jit(solution)/shard_map/all_gather | solution.py:78
  234.8 167.2 %reduce-scatter.2.cloned.1.call-start = ((), (), s32[]{:S(2)}) async-start(), calls=%async_computation.4 | async-start | bytes 2621440 | tf_op jit(solution)/shard_map/reduce_scatter | solution.py:194
  249.2 75.9 %copy-start.6 = (bf16[1,512,1024]{2,1,0:T(8,128)(2,1)S(1)}, bf16[1,512,1024]{2,1,0:T(8,128)(2,1)}, u32[]{:S(2)}) copy-start(bf16[1,512,1024]{2,1,0:T(8,128)(2,1)} %param.13) | copy-start | bytes 3145732
  328.0 0.7 copy-start.11
  328.0 0.7 copy-start.12
  329.1 10.2 %copy-start.7 = (bf16[512,1024]{1,0:T(8,128)(2,1)}, bf16[512,1024]{1,0:T(8,128)(2,1)S(1)}, u32[]{:S(2)}) copy-start(bf16[512,1024]{1,0:T(8,128)(2,1)S(1)} %add_convert_fusion) | copy-start | bytes 3145732
  339.3 0.7 copy-start.16
  342.2 62.4 %copy-start.13 = (f32[1024]{0:T(1024)S(1)}, f32[1024]{0:T(1024)}, u32[]{:S(2)}) copy-start(f32[1024]{0:T(1024)} %param.22) | copy-start | bytes 12292
  342.2 62.4 %copy-start.14 = (f32[1024]{0:T(1024)S(1)}, f32[1024]{0:T(1024)}, u32[]{:S(2)}) copy-start(f32[1024]{0:T(1024)} %param.21) | copy-start | bytes 12292
  342.2 37.6 %all-to-all-start = ((bf16[32,2,16,4,128]{4,3,2,1,0:T(4,128)(2,1)}), bf16[32,2,16,4,128]{4,3,2,1,0:T(4,128)(2,1)S(1)}, u32[]{:S(2)}, u32[]{:S(2)}) async-start(bf16[32,2,16,4,128]{4,3,2,1,0:T(4,128)(2,1)} %reshape.186), calls=%async_computation.1 | async-start | bytes 2097152 | tf_op jit(solution)/shard_map/all_to_all | solution.py:105
  401.9 5.7 %copy-start.1 = (bf16[1024,4,192]{0,2,1:T(8,128)(2,1)S(1)}, bf16[1024,4,192]{0,2,1:T(8,128)(2,1)}, u32[]{:S(2)}) copy-start(bf16[1024,4,192]{0,2,1:T(8,128)(2,1)} %param.14) | copy-start | bytes 4718596
Sparse Core Ops, SparseCore 0:
  11.4 72.0 all-gather.11
  158.2 71.8 all-gather.13
  234.3 35.6 all-gather.7
  271.9 53.1 all-gather.9
  339.5 62.4 reduce-scatter.1
